TPU v7x, 32 devices: a whole 2x2x4 slice. The times are simulated.
32 devices in a mesh: tm: 8 (over z, y), space: 4 (over x, core).
Axes of the slice: x: 2, y: 2, z: 4, core: 2. Of those that a mesh axis runs over, the one named last changes fastest.
Arguments:
- initial_guess: float32 [8, 1024, 1024], P('tm', 'space'), may hold values from -6 to 6
- start_field: float32 [1024, 1024], P('space'), may hold values from -6 to 6
- source_field: float32 [1024, 1024], P('space'), may hold values from -0.3 to 0.3
Outputs:
- final_states: float32 [8, 1024, 1024], P('tm', 'space')
All inputs are finite; a program needn't handle non-finite values.
Results may differ from a plain program's by a relative error of at most 0.00013.
Values sent between devices are 32-bit elements; how exact they have to be, the bound alone decides.
A program may use at most 64 MiB of HBM per device.

v0:
```python
import jax
import jax.numpy as jnp
from jax import lax
from jax.sharding import PartitionSpec as P

M = 16
decay_rate = 0.0005
spread_rate = 0.01


def shifted(value, axis, steps):
    count = lax.axis_size(axis)
    first, last = (max(0, -steps), min(count, count - steps))
    return lax.ppermute(value, axis, [(source, source + steps) for source in range(first, last)])


def cas_matrix(length):
    indices = jnp.arange(length, dtype=jnp.int32)
    product = indices[:, None] * indices[None, :] % length
    angles = 2.0 * jnp.pi / length * product.astype(jnp.float32)
    return jnp.cos(angles) + jnp.sin(angles)


def local_symbols(length, column_width):
    offset = lax.axis_index("space") * column_width
    row_modes = jnp.arange(length, dtype=jnp.int32).astype(jnp.float32)
    column_modes = (offset + jnp.arange(column_width, dtype=jnp.int32)).astype(jnp.float32)
    row_sines = jnp.sin(jnp.pi * row_modes / length) ** 2
    column_sines = jnp.sin(jnp.pi * column_modes / length) ** 2
    stiffness = 4.0 * (row_sines[:, None] + column_sines[None, :])
    fine_factor = 1.0 / (1.0 + decay_rate + spread_rate * stiffness)
    coarse_factor = 1.0 / (1.0 + M * decay_rate + M * spread_rate * stiffness)
    fine_power = jnp.ones_like(fine_factor)
    forcing_symbol = jnp.zeros_like(fine_factor)
    for substep in range(M):
        fine_power = fine_power * fine_factor
        forcing_symbol = forcing_symbol + fine_power
    return (fine_power, forcing_symbol, coarse_factor)


def forward(fields, kernel):
    along_rows = jnp.einsum("brj,jk->brk", fields, kernel, precision=lax.Precision.HIGHEST)
    columns = lax.all_to_all(along_rows, "space", split_axis=2, concat_axis=1, tiled=True)
    return jnp.einsum("ij,bjk->bik", kernel, columns, precision=lax.Precision.HIGHEST)


def inverse(spectra, kernel):
    length = kernel.shape[0]
    along_columns = jnp.einsum("ij,bjk->bik", kernel, spectra, precision=lax.Precision.HIGHEST)
    row_layout = lax.all_to_all(along_columns, "space", split_axis=1, concat_axis=2, tiled=True)
    restored = jnp.einsum("brj,jk->brk", row_layout, kernel, precision=lax.Precision.HIGHEST)
    return restored / float(length * length)


def previous(states, start_state, at_start):
    incoming = shifted(states[-1], "tm", 1)
    first_state = jnp.where(at_start, start_state, incoming)
    return jnp.concatenate([first_state[None], states[:-1]], axis=0)


def coarse_chain(residual_hat, coarse_factor):
    blocks = residual_hat.shape[0]
    running = jnp.zeros_like(residual_hat[0])
    position = 0
    running = coarse_factor * running + residual_hat[position]
    partial_value = [running]
    block_factor = coarse_factor**blocks
    relay_turns = lax.axis_size("tm") - 1

    def relay_turn(turn_index, carried):
        outgoing = block_factor * carried + running
        return shifted(outgoing, "tm", 1)

    entering = lax.fori_loop(0, relay_turns, relay_turn, jnp.zeros_like(running))
    lifting = jnp.ones_like(coarse_factor)
    position = 0
    lifting = lifting * coarse_factor
    errors = [partial_value[position] + lifting * entering]
    return jnp.stack(errors, axis=0)


def body(initial_guess, start_field, source_field):
    length = start_field.shape[1]
    column_width = length // lax.axis_size("space")
    kernel = cas_matrix(length)
    fine_power, forcing_symbol, coarse_factor = local_symbols(length, column_width)
    at_start = lax.axis_index("tm") == 0
    blocks = initial_guess.shape[0]
    stacked = jnp.concatenate([initial_guess, start_field[None], source_field[None]], axis=0)
    spectra = forward(stacked, kernel)
    states = spectra[:blocks]
    start_state = spectra[blocks]
    forcing = forcing_symbol * spectra[blocks + 1]
    relaxed = fine_power * previous(states, start_state, at_start) + forcing
    residual = fine_power * previous(relaxed, start_state, at_start) + forcing - relaxed
    states = relaxed + coarse_chain(residual, coarse_factor)
    return inverse(states, kernel)


def solution(mesh):
    return jax.shard_map(
        body,
        mesh=mesh,
        in_specs=(P("tm", "space", None), P("space", None), P("space", None)),
        out_specs=P("tm", "space", None),
        check_vma=False,
    )
```

profile of v0, /device:TPU:16, one launch (start us, length us, event | category | flops | bytes accessed | tf_op | source)
XLA Modules:
  0.0 402.9 jit_solution(6113995466226512795)
XLA Ops:
  2.1 28.3 %fusion.8 = f32[3,256,1024]{2,1,0:T(8,128)S(1)} fusion(f32[3,256,1024]{2,1,0:T(8,128)S(1)} %fusion.99), kind=kOutput, calls=%fused_computation.11 | convolution fusion | flops 9679405056 | bytes 6291456 | tf_op jit(solution)/shard_map/brj,jk->brk/dot_general | solution.py:42
  30.4 3.3 copy.19
  33.6 5.3 %all-to-all-start = ((f32[3,256,1024]{1,0,2:T(4,128)}), f32[3,256,1024]{1,0,2:T(4,128)}, u32[]{:S(2)}, u32[]{:S(2)}) async-start(f32[3,256,1024]{1,0,2:T(4,128)} %copy.19), calls=%async_computation | async-start | bytes 8388608 | tf_op jit(solution)/shard_map/all_to_all | solution.py:43
  38.9 17.5 %fusion.101 = f32[1024,1024,1]{1,0,2:T(8,128)} fusion(), kind=kLoop, calls=%fused_computation.10.clone.clone.clone.1 | loop fusion | flops 15728640 | bytes 4194304 | tf_op jit(solution)/shard_map/ij,bjk->bik/dot_general | solution.py:44
  56.4 30.7 %all-to-all-done = f32[3,256,1024]{1,0,2:T(4,128)} async-done(((f32[3,256,1024]{1,0,2:T(4,128)}), f32[3,256,1024]{1,0,2:T(4,128)}, u32[]{:S(2)}, u32[]{:S(2)}) %all-to-all-start) | async-done | bytes 3145760 | tf_op jit(solution)/shard_map/all_to_all | solution.py:43
  87.1 4.2 %copy.28 = f32[3,256,4,256]{1,2,3,0:T(4,128)S(1)} copy(f32[3,256,4,256]{1,0,3,2:T(4,128)} %bitcast.3) | data formatting | bytes 6291456 | tf_op jit(solution)/shard_map/all_to_all | solution.py:43
  91.3 3.1 all_to_all.27
  94.4 13.3 %fusion.20 = f32[3,1024,256]{1,2,0:T(8,128)S(1)} fusion(f32[3,1024,256]{1,2,0:T(8,128)} %all_to_all.27, f32[1024,1024,1]{1,0,2:T(8,128)} %fusion.101), kind=kOutput, calls=%fused_computation.27 | convolution fusion | flops 9663676416 | bytes 10485760 | tf_op jit(solution)/shard_map/ij,bjk->bik/dot_general | solution.py:44
  108.7 3.4 collective-permute-start.1
  112.2 24.2 %collective-permute-done.1 = f32[1024,256]{0,1:T(8,128)} collective-permute-done((f32[1024,256]{0,1:T(8,128)}, f32[1024,256]{0,1:T(8,128)}, u32[]{:S(2)}, u32[]{:S(2)}) %collective-permute-start.1) | collective-permute-done | bytes 1048608 | tf_op jit(solution)/shard_map/ppermute | solution.py:14
  136.4 2.6 multiply_add_fusion.1
  139.0 2.5 collective-permute-start.2
  141.5 24.0 %collective-permute-done.2 = f32[1024,256]{0,1:T(8,128)S(1)} collective-permute-done((f32[1024,256]{0,1:T(8,128)S(1)}, f32[1024,256]{0,1:T(8,128)S(1)}, u32[]{:S(2)}, u32[]{:S(2)}) %collective-permute-start.2) | collective-permute-done | bytes 1048608 | tf_op jit(solution)/shard_map/ppermute | solution.py:14
  169.2 166.4 %while.11 = (s32[]{:T(128)}, f32[1024,256]{1,0:T(8,128)S(1)}, f32[1024,256]{1,0:T(8,128)S(1)}, f32[256]{0:T(256)S(1)}, f32[1024]{0:T(1024)S(1)}, /*index=5*/s32[]{:T(128)}) while((s32[]{:T(128)}, f32[1024,256]{1,0:T(8,128)S(1)}, f32[1024,256]{1,0:T(8,128)S(1)}, f32[256]{0:T(256)S(1)}, f32[1024]{0:T(1024)S(1)}, ...), condition=%wide.region_1.2_spmd.clone, body=%wide.region_0.1_spmd.clone.sunk | while | flops 1572866 | bytes 7345261 | solution.py:74
  171.6 23.7 %collective-permute-done = f32[1024,256]{1,0:T(8,128)S(1)} collective-permute-done((f32[1024,256]{1,0:T(8,128)S(1)}, f32[1024,256]{1,0:T(8,128)S(1)}, u32[]{:S(2)}, u32[]{:S(2)}) %collective-permute-start) | collective-permute-done | bytes 1048608 | tf_op jit(solution)/shard_map/while/body/eval_jaxpr/ppermute | solution.py:14
  197.5 22.9 %collective-permute-done = f32[1024,256]{1,0:T(8,128)S(1)} collective-permute-done((f32[1024,256]{1,0:T(8,128)S(1)}, f32[1024,256]{1,0:T(8,128)S(1)}, u32[]{:S(2)}, u32[]{:S(2)}) %collective-permute-start) | collective-permute-done | bytes 1048608 | tf_op jit(solution)/shard_map/while/body/eval_jaxpr/ppermute | solution.py:14
  222.6 22.0 %collective-permute-done = f32[1024,256]{1,0:T(8,128)S(1)} collective-permute-done((f32[1024,256]{1,0:T(8,128)S(1)}, f32[1024,256]{1,0:T(8,128)S(1)}, u32[]{:S(2)}, u32[]{:S(2)}) %collective-permute-start) | collective-permute-done | bytes 1048608 | tf_op jit(solution)/shard_map/while/body/eval_jaxpr/ppermute | solution.py:14
  246.9 21.2 %collective-permute-done = f32[1024,256]{1,0:T(8,128)S(1)} collective-permute-done((f32[1024,256]{1,0:T(8,128)S(1)}, f32[1024,256]{1,0:T(8,128)S(1)}, u32[]{:S(2)}, u32[]{:S(2)}) %collective-permute-start) | collective-permute-done | bytes 1048608 | tf_op jit(solution)/shard_map/while/body/eval_jaxpr/ppermute | solution.py:14
  270.3 21.1 %collective-permute-done = f32[1024,256]{1,0:T(8,128)S(1)} collective-permute-done((f32[1024,256]{1,0:T(8,128)S(1)}, f32[1024,256]{1,0:T(8,128)S(1)}, u32[]{:S(2)}, u32[]{:S(2)}) %collective-permute-start) | collective-permute-done | bytes 1048608 | tf_op jit(solution)/shard_map/while/body/eval_jaxpr/ppermute | solution.py:14
  293.6 21.1 %collective-permute-done = f32[1024,256]{1,0:T(8,128)S(1)} collective-permute-done((f32[1024,256]{1,0:T(8,128)S(1)}, f32[1024,256]{1,0:T(8,128)S(1)}, u32[]{:S(2)}, u32[]{:S(2)}) %collective-permute-start) | collective-permute-done | bytes 1048608 | tf_op jit(solution)/shard_map/while/body/eval_jaxpr/ppermute | solution.py:14
  316.9 18.6 %collective-permute-done = f32[1024,256]{1,0:T(8,128)S(1)} collective-permute-done((f32[1024,256]{1,0:T(8,128)S(1)}, f32[1024,256]{1,0:T(8,128)S(1)}, u32[]{:S(2)}, u32[]{:S(2)}) %collective-permute-start) | collective-permute-done | bytes 1048608 | tf_op jit(solution)/shard_map/while/body/eval_jaxpr/ppermute | solution.py:14
  335.9 22.8 %fusion.27 = f32[1,1024,256]{1,2,0:T(8,128)S(1)} fusion(f32[1024,256]{0,1:T(8,128)} %copy-done, f32[1024,256]{0,1:T(8,128)} %subtract_add_fusion, f32[1024,256]{0,1:T(8,128)S(1)} %copy.23, f32[256]{0:T(256)S(1)} %get-tuple-element.130, f32[1024]{0:T(1024)S(1)} %get-tuple-element.129), kind=kOutput, calls=%fused_computation.34 | convolution fusion | flops 3238789120 | bytes 4199424 | tf_op jit(solution)/shard_map/ij,bjk->bik/dot_general | solution.py:49
  359.5 18.6 %all_to_all.33 = f32[1,1024,256]{2,0,1:T(1,128)S(1)} all-to-all(f32[1,1024,256]{2,0,1:T(1,128)S(1)} %copy.24), channel_id=1, replica_groups=mesh['tm'=8,'space'=4] {'space'}, dimensions={1} | all-to-all | bytes 2097152 | tf_op jit(solution)/shard_map/all_to_all | solution.py:50
  378.5 24.2 %fusion.29 = f32[1,256,1024]{2,1,0:T(8,128)} fusion(f32[256,1024]{0,1:T(8,128)S(1)} %bitcast.54), kind=kOutput, calls=%fused_computation.36 | convolution fusion | flops 3237216256 | bytes 2097152 | tf_op jit(solution)/shard_map/brj,jk->brk/dot_general | solution.py:51
  (27 shorter events, 23.7 us)
Async XLA Ops:
  33.6 53.5 %all-to-all-start = ((f32[3,256,1024]{1,0,2:T(4,128)}), f32[3,256,1024]{1,0,2:T(4,128)}, u32[]{:S(2)}, u32[]{:S(2)}) async-start(f32[3,256,1024]{1,0,2:T(4,128)} %copy.19), calls=%async_computation | async-start | bytes 8388608 | tf_op jit(solution)/shard_map/all_to_all | solution.py:43
  108.7 27.7 %collective-permute-start.1 = (f32[1024,256]{0,1:T(8,128)}, f32[1024,256]{0,1:T(8,128)}, u32[]{:S(2)}, u32[]{:S(2)}) collective-permute-start(f32[1024,256]{0,1:T(8,128)} %slice_bitcast_fusion.1), channel_id=1, source_target_pairs={{0,4},{4,8},{8,12},{12,16},{16,20},{20,24},{24,28},{1,5},{5,9},{9,... | collective-permute-start | bytes 3145736 | tf_op jit(solution)/shard_map/ppermute | solution.py:14
  139.0 26.5 %copy-start = (f32[1024,256]{0,1:T(8,128)}, f32[1024,256]{0,1:T(8,128)S(1)}, u32[]{:S(2)}) copy-start(f32[1024,256]{0,1:T(8,128)S(1)} %get-tuple-element.72) | copy-start | bytes 3145732
  139.0 26.5 %collective-permute-start.2 = (f32[1024,256]{0,1:T(8,128)S(1)}, f32[1024,256]{0,1:T(8,128)S(1)}, u32[]{:S(2)}, u32[]{:S(2)}) collective-permute-start(f32[1024,256]{0,1:T(8,128)S(1)} %get-tuple-element.72), channel_id=1, source_target_pairs={{0,4},{4,8},{8,12},{12,16},{16,20},{20,24},{24,28},{1,5},{5,9},{9,... | collective-permute-start | bytes 3145736 | tf_op jit(solution)/shard_map/ppermute | solution.py:14
  169.6 25.7 %collective-permute-start = (f32[1024,256]{1,0:T(8,128)S(1)}, f32[1024,256]{1,0:T(8,128)S(1)}, u32[]{:S(2)}, u32[]{:S(2)}) collective-permute-start(f32[1024,256]{1,0:T(8,128)S(1)} %fusion.104), channel_id=1, source_target_pairs={{0,4},{4,8},{8,12},{12,16},{16,20},{20,24},{24,28},{1,5},{5,9},{9,... | collective-permute-start | bytes 3145736 | tf_op jit(solution)/shard_map/while/body/eval_jaxpr/ppermute | solution.py:14
  195.6 24.8 %collective-permute-start = (f32[1024,256]{1,0:T(8,128)S(1)}, f32[1024,256]{1,0:T(8,128)S(1)}, u32[]{:S(2)}, u32[]{:S(2)}) collective-permute-start(f32[1024,256]{1,0:T(8,128)S(1)} %fusion.104), channel_id=1, source_target_pairs={{0,4},{4,8},{8,12},{12,16},{16,20},{20,24},{24,28},{1,5},{5,9},{9,... | collective-permute-start | bytes 3145736 | tf_op jit(solution)/shard_map/while/body/eval_jaxpr/ppermute | solution.py:14
  220.7 24.0 %collective-permute-start = (f32[1024,256]{1,0:T(8,128)S(1)}, f32[1024,256]{1,0:T(8,128)S(1)}, u32[]{:S(2)}, u32[]{:S(2)}) collective-permute-start(f32[1024,256]{1,0:T(8,128)S(1)} %fusion.104), channel_id=1, source_target_pairs={{0,4},{4,8},{8,12},{12,16},{16,20},{20,24},{24,28},{1,5},{5,9},{9,... | collective-permute-start | bytes 3145736 | tf_op jit(solution)/shard_map/while/body/eval_jaxpr/ppermute | solution.py:14
  245.0 23.1 %collective-permute-start = (f32[1024,256]{1,0:T(8,128)S(1)}, f32[1024,256]{1,0:T(8,128)S(1)}, u32[]{:S(2)}, u32[]{:S(2)}) collective-permute-start(f32[1024,256]{1,0:T(8,128)S(1)} %fusion.104), channel_id=1, source_target_pairs={{0,4},{4,8},{8,12},{12,16},{16,20},{20,24},{24,28},{1,5},{5,9},{9,... | collective-permute-start | bytes 3145736 | tf_op jit(solution)/shard_map/while/body/eval_jaxpr/ppermute | solution.py:14
  268.4 23.0 %collective-permute-start = (f32[1024,256]{1,0:T(8,128)S(1)}, f32[1024,256]{1,0:T(8,128)S(1)}, u32[]{:S(2)}, u32[]{:S(2)}) collective-permute-start(f32[1024,256]{1,0:T(8,128)S(1)} %fusion.104), channel_id=1, source_target_pairs={{0,4},{4,8},{8,12},{12,16},{16,20},{20,24},{24,28},{1,5},{5,9},{9,... | collective-permute-start | bytes 3145736 | tf_op jit(solution)/shard_map/while/body/eval_jaxpr/ppermute | solution.py:14
  291.7 23.0 %collective-permute-start = (f32[1024,256]{1,0:T(8,128)S(1)}, f32[1024,256]{1,0:T(8,128)S(1)}, u32[]{:S(2)}, u32[]{:S(2)}) collective-permute-start(f32[1024,256]{1,0:T(8,128)S(1)} %fusion.104), channel_id=1, source_target_pairs={{0,4},{4,8},{8,12},{12,16},{16,20},{20,24},{24,28},{1,5},{5,9},{9,... | collective-permute-start | bytes 3145736 | tf_op jit(solution)/shard_map/while/body/eval_jaxpr/ppermute | solution.py:14
  315.0 20.5 %collective-permute-start = (f32[1024,256]{1,0:T(8,128)S(1)}, f32[1024,256]{1,0:T(8,128)S(1)}, u32[]{:S(2)}, u32[]{:S(2)}) collective-permute-start(f32[1024,256]{1,0:T(8,128)S(1)} %fusion.104), channel_id=1, source_target_pairs={{0,4},{4,8},{8,12},{12,16},{16,20},{20,24},{24,28},{1,5},{5,9},{9,... | collective-permute-start | bytes 3145736 | tf_op jit(solution)/shard_map/while/body/eval_jaxpr/ppermute | solution.py:14
where the time goes:
time: 409 us; the launch traced here: 403 us
  waiting for transfers between devices  229 us (56%)
  matrix products  88.5 us (22%)
  other arithmetic  26.2 us (6%)
  starting transfers between devices  24.7 us (6%)
  blocking collectives  18.6 us (5%)
  local copies, waits for them, and re-layouts  14.7 us (4%)
    ppermute x9, waiting for transfers between devices, shifted(): lax.ppermute(value, axis, [(source, source + steps) for source in range(f...  199 us
    all_to_all x1, waiting for transfers between devices, forward(): lax.all_to_all(along_rows, 'space', split_axis=2, concat_axis=1, tiled=True)  30.7 us
    dot_general x1, matrix products, forward(): jnp.einsum('brj,jk->brk', fields, kernel, precision=lax.Precision.HIGHEST)  28.3 us
    dot_general x1, matrix products, inverse(): jnp.einsum('brj,jk->brk', row_layout, kernel, precision=lax.Precision.HIG...  24.2 us
    dot_general x1, matrix products, inverse(): jnp.einsum('ij,bjk->bik', kernel, spectra, precision=lax.Precision.HIGHEST)  22.8 us
    ppermute x9, starting transfers between devices, shifted(): lax.ppermute(value, axis, [(source, source + steps) for source in range(f...  19.4 us
    all_to_all x1, blocking collectives, inverse(): lax.all_to_all(along_columns, 'space', split_axis=1, concat_axis=2, tiled...  18.6 us
    dot_general x1, other arithmetic, forward(): jnp.einsum('ij,bjk->bik', kernel, columns, precision=lax.Precision.HIGHEST)  17.5 us
  transfers between devices with their start and end apart: 10, of which 10 were waited for; matrix products, arithmetic and copies ran while one was open for 4% of the time, Pallas kernels for 0%

commit v1 on v0

--- a/solution.py
+++ b/solution.py
@@ -40,7 +40,12 @@
 
 def forward(fields, kernel):
     along_rows = jnp.einsum("brj,jk->brk", fields, kernel, precision=lax.Precision.HIGHEST)
-    columns = lax.all_to_all(along_rows, "space", split_axis=2, concat_axis=1, tiled=True)
+    columns = jnp.concatenate(
+        lax.all_to_all(
+            jnp.stack(jnp.split(along_rows, lax.axis_size("space"), axis=2)), "space", 0, 0
+        ),
+        axis=1,
+    )
     return jnp.einsum("ij,bjk->bik", kernel, columns, precision=lax.Precision.HIGHEST)
 
 

time: 409 us -> 399 us (0.976)
  waiting for transfers between devices: 229 us -> 218 us
  local copies, waits for them, and re-layouts: 14.7 us -> 6.67 us
  matrix products: 88.5 us -> 95.8 us
    all_to_all x1, waiting for transfers between devices: 30.7 us -> 19.2 us  [forward(): lax.all_to_all(jnp.stack(jnp.split(along_rows, lax.axis_size('space'), ax...]
    dot_general x1, matrix products: 13.3 us -> 20.6 us  [forward(): jnp.einsum('ij,bjk->bik', kernel, columns, precision=lax.Precision.HIGHEST)]
    all_to_all x2 -> x0, local copies, waits for them, and re-layouts: 7.27 us -> none  [forward(): lax.all_to_all(along_rows, 'space', split_axis=2, concat_axis=1, tiled=True)]
  transfers between devices with their start and end apart: 10 -> 10, of which waited for: 10 -> 10; matrix products, arithmetic and copies ran while one was open for 4% -> 5% of each run, Pallas kernels for 0% -> 0%
where the time goes in v1:
time: 399 us; the launch traced here: 392 us
  waiting for transfers between devices  218 us (55%)
  matrix products  95.8 us (24%)
  other arithmetic  28.4 us (7%)
  starting transfers between devices  23.1 us (6%)
  blocking collectives  18.6 us (5%)
  local copies, waits for them, and re-layouts  6.67 us (2%)
    ppermute x9, waiting for transfers between devices, shifted(): lax.ppermute(value, axis, [(source, source + steps) for source in range(f...  199 us
    dot_general x1, matrix products, forward(): jnp.einsum('brj,jk->brk', fields, kernel, precision=lax.Precision.HIGHEST)  28.3 us
    dot_general x1, matrix products, inverse(): jnp.einsum('brj,jk->brk', row_layout, kernel, precision=lax.Precision.HIG...  24.2 us
    dot_general x1, matrix products, inverse(): jnp.einsum('ij,bjk->bik', kernel, spectra, precision=lax.Precision.HIGHEST)  22.8 us
    dot_general x1, matrix products, forward(): jnp.einsum('ij,bjk->bik', kernel, columns, precision=lax.Precision.HIGHEST)  20.6 us
    ppermute x9, starting transfers between devices, shifted(): lax.ppermute(value, axis, [(source, source + steps) for source in range(f...  19.4 us
    all_to_all x1, waiting for transfers between devices, forward(): lax.all_to_all(jnp.stack(jnp.split(along_rows, lax.axis_size('space'), ax...  19.2 us
    all_to_all x1, blocking collectives, inverse(): lax.all_to_all(along_columns, 'space', split_axis=1, concat_axis=2, tiled...  18.6 us
  transfers between devices with their start and end apart: 10, of which 10 were waited for; matrix products, arithmetic and copies ran while one was open for 5% of the time, Pallas kernels for 0%

profile of v1, /device:TPU:16, one launch (start us, length us, event | category | flops | bytes accessed | tf_op | source)
XLA Modules:
  0.0 391.6 jit_solution(5295262825563427930)
XLA Ops:
  0.0 2.1 fusion.99
  2.1 28.3 %fusion.8 = f32[3,256,1024]{2,1,0:T(8,128)S(1)} fusion(f32[3,256,1024]{2,1,0:T(8,128)S(1)} %fusion.99), kind=kOutput, calls=%fused_computation.11 | convolution fusion | flops 9679405056 | bytes 6291456 | tf_op jit(solution)/shard_map/brj,jk->brk/dot_general | solution.py:42
  30.7 2.1 pad_maximum_fusion
  32.7 3.7 all-to-all-start
  36.5 17.7 %fusion.101 = f32[1024,1024,1]{1,0,2:T(8,128)} fusion(), kind=kLoop, calls=%fused_computation.10.clone.clone.clone.1 | loop fusion | flops 15728640 | bytes 4194304 | tf_op jit(solution)/shard_map/ij,bjk->bik/dot_general | solution.py:49
  54.1 19.2 %all-to-all-done = f32[4,3,256,256]{3,2,1,0:T(8,128)S(1)} async-done(((f32[4,3,256,256]{3,2,1,0:T(8,128)}), f32[4,3,256,256]{3,2,1,0:T(8,128)S(1)}, u32[]{:S(2)}, u32[]{:S(2)}) %all-to-all-start) | async-done | bytes 3145760 | tf_op jit(solution)/shard_map/all_to_all | solution.py:44
  75.5 20.6 %fusion.20 = f32[3,1024,256]{1,2,0:T(8,128)S(1)} fusion(f32[3,1024,256]{2,1,0:T(8,128)S(1)} %bitcast.57, f32[1024,1024,1]{1,0,2:T(8,128)S(1)} %copy-done), kind=kOutput, calls=%fused_computation.27 | convolution fusion | flops 9663676416 | bytes 10485760 | tf_op jit(solution)/shard_map/ij,bjk->bik/dot_general | solution.py:49
  97.1 3.4 collective-permute-start.1
  100.7 24.2 %collective-permute-done.1 = f32[1024,256]{0,1:T(8,128)} collective-permute-done((f32[1024,256]{0,1:T(8,128)}, f32[1024,256]{0,1:T(8,128)}, u32[]{:S(2)}, u32[]{:S(2)}) %collective-permute-start.1) | collective-permute-done | bytes 1048608 | tf_op jit(solution)/shard_map/ppermute | solution.py:14
  124.8 2.6 multiply_add_fusion.1
  127.4 2.5 collective-permute-start.2
  130.0 24.0 %collective-permute-done.2 = f32[1024,256]{0,1:T(8,128)S(1)} collective-permute-done((f32[1024,256]{0,1:T(8,128)S(1)}, f32[1024,256]{0,1:T(8,128)S(1)}, u32[]{:S(2)}, u32[]{:S(2)}) %collective-permute-start.2) | collective-permute-done | bytes 1048608 | tf_op jit(solution)/shard_map/ppermute | solution.py:14
  154.0 2.0 subtract_add_fusion
  157.6 166.7 %while.11 = (s32[]{:T(128)}, f32[1024,256]{1,0:T(8,128)S(1)}, f32[1024,256]{1,0:T(8,128)S(1)}, f32[256]{0:T(256)S(1)}, f32[1024]{0:T(1024)S(1)}, /*index=5*/s32[]{:T(128)}) while((s32[]{:T(128)}, f32[1024,256]{1,0:T(8,128)S(1)}, f32[1024,256]{1,0:T(8,128)S(1)}, f32[256]{0:T(256)S(1)}, f32[1024]{0:T(1024)S(1)}, ...), condition=%wide.region_1.2_spmd.clone, body=%wide.region_0.1_spmd.clone.sunk | while | flops 1572866 | bytes 7345261 | solution.py:79
  160.2 23.8 %collective-permute-done = f32[1024,256]{1,0:T(8,128)S(1)} collective-permute-done((f32[1024,256]{1,0:T(8,128)S(1)}, f32[1024,256]{1,0:T(8,128)S(1)}, u32[]{:S(2)}, u32[]{:S(2)}) %collective-permute-start) | collective-permute-done | bytes 1048608 | tf_op jit(solution)/shard_map/while/body/eval_jaxpr/ppermute | solution.py:14
  186.2 22.9 %collective-permute-done = f32[1024,256]{1,0:T(8,128)S(1)} collective-permute-done((f32[1024,256]{1,0:T(8,128)S(1)}, f32[1024,256]{1,0:T(8,128)S(1)}, u32[]{:S(2)}, u32[]{:S(2)}) %collective-permute-start) | collective-permute-done | bytes 1048608 | tf_op jit(solution)/shard_map/while/body/eval_jaxpr/ppermute | solution.py:14
  211.3 22.0 %collective-permute-done = f32[1024,256]{1,0:T(8,128)S(1)} collective-permute-done((f32[1024,256]{1,0:T(8,128)S(1)}, f32[1024,256]{1,0:T(8,128)S(1)}, u32[]{:S(2)}, u32[]{:S(2)}) %collective-permute-start) | collective-permute-done | bytes 1048608 | tf_op jit(solution)/shard_map/while/body/eval_jaxpr/ppermute | solution.py:14
  235.6 21.2 %collective-permute-done = f32[1024,256]{1,0:T(8,128)S(1)} collective-permute-done((f32[1024,256]{1,0:T(8,128)S(1)}, f32[1024,256]{1,0:T(8,128)S(1)}, u32[]{:S(2)}, u32[]{:S(2)}) %collective-permute-start) | collective-permute-done | bytes 1048608 | tf_op jit(solution)/shard_map/while/body/eval_jaxpr/ppermute | solution.py:14
  259.0 21.1 %collective-permute-done = f32[1024,256]{1,0:T(8,128)S(1)} collective-permute-done((f32[1024,256]{1,0:T(8,128)S(1)}, f32[1024,256]{1,0:T(8,128)S(1)}, u32[]{:S(2)}, u32[]{:S(2)}) %collective-permute-start) | collective-permute-done | bytes 1048608 | tf_op jit(solution)/shard_map/while/body/eval_jaxpr/ppermute | solution.py:14
  282.3 21.1 %collective-permute-done = f32[1024,256]{1,0:T(8,128)S(1)} collective-permute-done((f32[1024,256]{1,0:T(8,128)S(1)}, f32[1024,256]{1,0:T(8,128)S(1)}, u32[]{:S(2)}, u32[]{:S(2)}) %collective-permute-start) | collective-permute-done | bytes 1048608 | tf_op jit(solution)/shard_map/while/body/eval_jaxpr/ppermute | solution.py:14
  305.6 18.6 %collective-permute-done = f32[1024,256]{1,0:T(8,128)S(1)} collective-permute-done((f32[1024,256]{1,0:T(8,128)S(1)}, f32[1024,256]{1,0:T(8,128)S(1)}, u32[]{:S(2)}, u32[]{:S(2)}) %collective-permute-start) | collective-permute-done | bytes 1048608 | tf_op jit(solution)/shard_map/while/body/eval_jaxpr/ppermute | solution.py:14
  324.6 22.8 %fusion.27 = f32[1,1024,256]{1,2,0:T(8,128)S(1)} fusion(f32[1024,256]{0,1:T(8,128)} %copy-done.1, f32[1024,256]{0,1:T(8,128)} %subtract_add_fusion, f32[1024,256]{0,1:T(8,128)S(1)} %copy.23, f32[256]{0:T(256)S(1)} %get-tuple-element.135, f32[1024]{0:T(1024)S(1)} %get-tuple-element.134), kind=kOutput, calls=%fused_computation.34 | convolution fusion | flops 3238789120 | bytes 4199424 | tf_op jit(solution)/shard_map/ij,bjk->bik/dot_general | solution.py:54
  348.2 18.6 %all_to_all.20 = f32[1,1024,256]{2,0,1:T(1,128)S(1)} all-to-all(f32[1,1024,256]{2,0,1:T(1,128)S(1)} %copy.24), channel_id=1, replica_groups=mesh['tm'=8,'space'=4] {'space'}, dimensions={1} | all-to-all | bytes 2097152 | tf_op jit(solution)/shard_map/all_to_all | solution.py:55
  367.3 24.2 %fusion.29 = f32[1,256,1024]{2,1,0:T(8,128)} fusion(f32[256,1024]{0,1:T(8,128)S(1)} %bitcast.59), kind=kOutput, calls=%fused_computation.36 | convolution fusion | flops 3237216256 | bytes 2097152 | tf_op jit(solution)/shard_map/brj,jk->brk/dot_general | solution.py:56
  (29 shorter events, 22.2 us)
Async XLA Ops:
  32.7 40.6 %all-to-all-start = ((f32[4,3,256,256]{3,2,1,0:T(8,128)}), f32[4,3,256,256]{3,2,1,0:T(8,128)S(1)}, u32[]{:S(2)}, u32[]{:S(2)}) async-start(f32[4,3,256,256]{3,2,1,0:T(8,128)} %pad_maximum_fusion), calls=%async_computation | async-start | bytes 6291456 | tf_op jit(solution)/shard_map/all_to_all | solution.py:44
  73.3 2.2 copy-start
  97.1 27.7 %collective-permute-start.1 = (f32[1024,256]{0,1:T(8,128)}, f32[1024,256]{0,1:T(8,128)}, u32[]{:S(2)}, u32[]{:S(2)}) collective-permute-start(f32[1024,256]{0,1:T(8,128)} %slice_bitcast_fusion.1), channel_id=1, source_target_pairs={{0,4},{4,8},{8,12},{12,16},{16,20},{20,24},{24,28},{1,5},{5,9},{9,... | collective-permute-start | bytes 3145736 | tf_op jit(solution)/shard_map/ppermute | solution.py:14
  127.4 26.6 %copy-start.1 = (f32[1024,256]{0,1:T(8,128)}, f32[1024,256]{0,1:T(8,128)S(1)}, u32[]{:S(2)}) copy-start(f32[1024,256]{0,1:T(8,128)S(1)} %get-tuple-element.72) | copy-start | bytes 3145732
  127.4 26.5 %collective-permute-start.2 = (f32[1024,256]{0,1:T(8,128)S(1)}, f32[1024,256]{0,1:T(8,128)S(1)}, u32[]{:S(2)}, u32[]{:S(2)}) collective-permute-start(f32[1024,256]{0,1:T(8,128)S(1)} %get-tuple-element.72), channel_id=1, source_target_pairs={{0,4},{4,8},{8,12},{12,16},{16,20},{20,24},{24,28},{1,5},{5,9},{9,... | collective-permute-start | bytes 3145736 | tf_op jit(solution)/shard_map/ppermute | solution.py:14
  158.3 25.7 %collective-permute-start = (f32[1024,256]{1,0:T(8,128)S(1)}, f32[1024,256]{1,0:T(8,128)S(1)}, u32[]{:S(2)}, u32[]{:S(2)}) collective-permute-start(f32[1024,256]{1,0:T(8,128)S(1)} %fusion.104), channel_id=1, source_target_pairs={{0,4},{4,8},{8,12},{12,16},{16,20},{20,24},{24,28},{1,5},{5,9},{9,... | collective-permute-start | bytes 3145736 | tf_op jit(solution)/shard_map/while/body/eval_jaxpr/ppermute | solution.py:14
  184.3 24.8 %collective-permute-start = (f32[1024,256]{1,0:T(8,128)S(1)}, f32[1024,256]{1,0:T(8,128)S(1)}, u32[]{:S(2)}, u32[]{:S(2)}) collective-permute-start(f32[1024,256]{1,0:T(8,128)S(1)} %fusion.104), channel_id=1, source_target_pairs={{0,4},{4,8},{8,12},{12,16},{16,20},{20,24},{24,28},{1,5},{5,9},{9,... | collective-permute-start | bytes 3145736 | tf_op jit(solution)/shard_map/while/body/eval_jaxpr/ppermute | solution.py:14
  209.4 24.0 %collective-permute-start = (f32[1024,256]{1,0:T(8,128)S(1)}, f32[1024,256]{1,0:T(8,128)S(1)}, u32[]{:S(2)}, u32[]{:S(2)}) collective-permute-start(f32[1024,256]{1,0:T(8,128)S(1)} %fusion.104), channel_id=1, source_target_pairs={{0,4},{4,8},{8,12},{12,16},{16,20},{20,24},{24,28},{1,5},{5,9},{9,... | collective-permute-start | bytes 3145736 | tf_op jit(solution)/shard_map/while/body/eval_jaxpr/ppermute | solution.py:14
  233.7 23.1 %collective-permute-start = (f32[1024,256]{1,0:T(8,128)S(1)}, f32[1024,256]{1,0:T(8,128)S(1)}, u32[]{:S(2)}, u32[]{:S(2)}) collective-permute-start(f32[1024,256]{1,0:T(8,128)S(1)} %fusion.104), channel_id=1, source_target_pairs={{0,4},{4,8},{8,12},{12,16},{16,20},{20,24},{24,28},{1,5},{5,9},{9,... | collective-permute-start | bytes 3145736 | tf_op jit(solution)/shard_map/while/body/eval_jaxpr/ppermute | solution.py:14
  257.1 23.0 %collective-permute-start = (f32[1024,256]{1,0:T(8,128)S(1)}, f32[1024,256]{1,0:T(8,128)S(1)}, u32[]{:S(2)}, u32[]{:S(2)}) collective-permute-start(f32[1024,256]{1,0:T(8,128)S(1)} %fusion.104), channel_id=1, source_target_pairs={{0,4},{4,8},{8,12},{12,16},{16,20},{20,24},{24,28},{1,5},{5,9},{9,... | collective-permute-start | bytes 3145736 | tf_op jit(solution)/shard_map/while/body/eval_jaxpr/ppermute | solution.py:14
  280.4 23.0 %collective-permute-start = (f32[1024,256]{1,0:T(8,128)S(1)}, f32[1024,256]{1,0:T(8,128)S(1)}, u32[]{:S(2)}, u32[]{:S(2)}) collective-permute-start(f32[1024,256]{1,0:T(8,128)S(1)} %fusion.104), channel_id=1, source_target_pairs={{0,4},{4,8},{8,12},{12,16},{16,20},{20,24},{24,28},{1,5},{5,9},{9,... | collective-permute-start | bytes 3145736 | tf_op jit(solution)/shard_map/while/body/eval_jaxpr/ppermute | solution.py:14
  303.7 20.6 %collective-permute-start = (f32[1024,256]{1,0:T(8,128)S(1)}, f32[1024,256]{1,0:T(8,128)S(1)}, u32[]{:S(2)}, u32[]{:S(2)}) collective-permute-start(f32[1024,256]{1,0:T(8,128)S(1)} %fusion.104), channel_id=1, source_target_pairs={{0,4},{4,8},{8,12},{12,16},{16,20},{20,24},{24,28},{1,5},{5,9},{9,... | collective-permute-start | bytes 3145736 | tf_op jit(solution)/shard_map/while/body/eval_jaxpr/ppermute | solution.py:14
